TPU v7x, 128 devices: a whole 4x4x4 slice. The times are simulated.
128 devices in a mesh: row: 8 (over z, core), col: 16 (over y, x).
Axes of the slice: x: 4, y: 4, z: 4, core: 2. Of those that a mesh axis runs over, the one named last changes fastest.
Arguments:
- a_blocks: bfloat16 [1024, 16, 4, 4096], P('row', 'col'), may hold values from -0.125 to 0.125
- a_index: int32 [1024, 16, 4], P('row', 'col'), may hold values from 0 to 63, as said below
- p_blocks: bfloat16 [64, 16, 4, 4096], P('row', 'col'), may hold values from -2 to 2
- p_index: int32 [64, 16, 4], P('row', 'col'), may hold values from 0 to 127, as said below
- ap_index: int32 [1024, 8], P('row'), may hold values from 0 to 127, as said below
- coarse_index: int32 [128, 8], replicated, may hold values from 0 to 127, as said below
Outputs:
- ap_out: bfloat16 [64, 16, 8, 4096], P('row', 'col')
- coarse_out: float32 [128, 8, 4096], P(('row', 'col'))
Inputs may be any that keep to these rules, and one draw needn't show every extreme that they name: `a_index`: within one (i, c) the 4 entries are distinct. `p_index`: within one row the 4 entries are distinct. `ap_index`: within one row the 8 entries are distinct. `coarse_index`: within one row the 8 entries are distinct.
All inputs are finite; a program needn't handle non-finite values.
Results may differ from a plain program's by a relative error of at most 0.0029.
Values may be sent and summed in bfloat16 or wider, within the bound.
No kernel may reach another device: no remote copies, remote signals or barrier semaphores. Data moves between devices by JAX's collectives and lax.ppermute only.
A program may use at most 320 MiB of HBM per device.

v0:
```python
import jax
import jax.numpy as jnp
from jax import lax
from jax.sharding import PartitionSpec as P

B = 64
KA = 4
KP = 4
KAP = 8
KC = 8


def shards(a_blocks, a_index, p_blocks, p_index, ap_index, coarse_index):
    row_count = a_blocks.shape[0]
    own_rows = p_blocks.shape[0]
    col_count = lax.axis_size("col")
    gathered_vals, gathered_cols = (
        lax.all_gather(p_blocks, "row", axis=0, tiled=True),
        lax.all_gather(p_index, "row", axis=0, tiled=True),
    )
    group_vals = gathered_vals[:, 0]
    group_cols = gathered_cols[:, 0]
    partial_value = jnp.zeros((row_count, KAP, B, B), jnp.float32)
    for position in range(KA):
        fine_cols = a_index[:, 0, position]
        picked = jnp.take(group_vals, fine_cols, axis=0)
        picked_cols = jnp.take(group_cols, fine_cols, axis=0)
        select = (picked_cols[:, :, None] == ap_index[:, None, :]).astype(jnp.bfloat16)
        chosen = jnp.einsum("rms,rmx->rsx", select, picked, preferred_element_type=jnp.float32)
        chosen = chosen.astype(jnp.bfloat16).reshape(row_count, KAP, B, B)
        jac_block = a_blocks[:, 0, position].reshape(row_count, B, B)
        partial_value = partial_value + jnp.einsum(
            "rax,rsxb->rsab", jac_block, chosen, preferred_element_type=jnp.float32
        )
    summed = lax.psum_scatter(
        partial_value.reshape(own_rows, col_count, KAP, B * B),
        "col",
        scatter_dimension=1,
        tiled=True,
    )
    ap_blocks = summed.astype(jnp.bfloat16)
    own_col = lax.axis_index("col")
    local_slots = lax.dynamic_index_in_dim(
        ap_index.reshape(own_rows, col_count, KAP), own_col, 1, keepdims=False
    )
    prolong_own = p_blocks[:, 0].reshape(own_rows, KP, B, B)
    ap_own = ap_blocks[:, 0].reshape(own_rows, KAP, B, B)
    terms = jnp.einsum("umxa,usxb->umsab", prolong_own, ap_own, preferred_element_type=jnp.float32)
    coarse_rows = p_index[:, 0]
    targets = jnp.take(coarse_index, coarse_rows, axis=0)
    equal = targets[:, :, None, :] == local_slots[:, None, :, None]
    where_slot = jnp.sum(
        jnp.where(equal, lax.broadcasted_iota(jnp.int32, equal.shape, 3), 0), axis=3
    )
    found = jnp.any(equal, axis=3)
    coarse_total = coarse_index.shape[0]
    flat = jnp.where(found, coarse_rows[:, :, None] * KC + where_slot, coarse_total * KC).reshape(
        -1
    )
    coarse_terms = jnp.zeros((coarse_total * KC, B * B), jnp.float32)
    coarse_terms = coarse_terms.at[flat].add(terms.reshape(-1, B * B), mode="drop")
    coarse_terms = coarse_terms.reshape(coarse_total, KC, B * B)
    coarse_out = lax.psum_scatter(coarse_terms, ("row", "col"), scatter_dimension=0, tiled=True)
    return (ap_blocks, coarse_out)


def solution(mesh):
    placed = (
        P("row", "col", None, None),
        P("row", "col", None),
        P("row", "col", None, None),
        P("row", "col", None),
        P("row", None),
        P(),
    )
    return jax.shard_map(
        shards,
        mesh=mesh,
        in_specs=placed,
        out_specs=(P("row", "col", None, None), P(("row", "col"), None, None)),
        check_vma=False,
    )
```

profile of v0, /device:TPU:0, one launch (start us, length us, event | category | flops | bytes accessed | tf_op | source)
XLA Modules:
  0.0 1584.5 jit_solution(6816756833203105616)
XLA Ops:
  7.2 0.7 all-gather.2.cloned.1.call-update
  8.0 2.2 reshape.250
  10.2 0.8 copy.72
  11.0 0.8 reshape.137
  11.7 1.4 compare_and_fusion
  13.1 0.8 copy.71
  13.9 14.2 all_gather.6
  28.1 0.6 gather_fusion.3
  28.7 0.6 gather_fusion.1
  29.4 16.5 %fusion.33 = (bf16[128,1,1,4096]{3,2,1,0:T(2,128)(2,1)S(1)}, bf16[128,1,1,4096]{3,2,1,0:T(2,128)(2,1)}, bf16[128,1,1,4096]{3,2,1,0:T(2,128)(2,1)}, bf16[128,1,1,4096]{3,2,1,0:T(2,128)(2,1)}) fusion(bf16[128,1,4,4096]{3,2,1,0:T(4,128)(2,1)} %param.10), kind=kLoop, calls=%fused_computation.77 | loop fusion | bytes 8388608 | tf_op jit(solution)/shard_map/slice | solution.py:31
  45.9 5.0 copy.115
  51.0 3.8 copy.97
  54.7 5.0 copy.116
  59.8 3.8 copy.98
  63.5 0.6 gather_fusion.5
  64.2 0.6 gather_fusion.7
  64.9 5.0 copy.117
  69.9 3.8 copy.99
  73.7 2.6 copy.118
  76.3 3.8 copy.100
  80.2 0.1 copy.93
  80.3 0.8 copy.92
  81.1 0.1 copy.91
  81.2 0.1 reshape.206
  81.3 0.1 copy.90
  81.4 0.1 copy.94
  81.5 0.6 gather_fusion
  82.2 0.7 compare_reduce_fusion
  82.9 0.7 fusion.20
  83.6 0.1 select_n.76
  83.8 1.3 dynamic-slice
  85.0 0.5 compare_select_fusion.1
  85.6 0.7 broadcast_select_fusion.2
  86.3 0.8 broadcast_select_fusion
  87.1 9.5 gather_fusion.2
  96.6 7.6 gather_fusion.4
  104.3 7.5 gather_fusion.6
  111.8 7.8 gather_fusion.8
  119.5 7.7 convolution_convert_fusion.3
  127.2 12.5 copy.73
  139.7 40.6 %copy.75 = bf16[128,8,64,64]{2,3,1,0:T(8,128)(2,1)} copy(bf16[128,8,64,64]{0,3,2,1:T(8,128)(2,1)} %bitcast.83) | data formatting | bytes 16777216 | tf_op jit(solution)/shard_map/reshape | solution.py:30
  180.3 7.7 convolution_convert_fusion.2
  188.0 12.5 copy.77
  200.4 29.2 %copy.79 = bf16[128,8,64,64]{2,3,1,0:T(8,128)(2,1)} copy(bf16[128,8,64,64]{0,3,2,1:T(8,128)(2,1)} %bitcast.84) | data formatting | bytes 16777216 | tf_op jit(solution)/shard_map/reshape | solution.py:30
  229.7 7.6 convolution_convert_fusion.1
  237.3 12.5 copy.81
  249.8 29.2 %copy.83 = bf16[128,8,64,64]{2,3,1,0:T(8,128)(2,1)} copy(bf16[128,8,64,64]{0,3,2,1:T(8,128)(2,1)} %bitcast.85) | data formatting | bytes 16777216 | tf_op jit(solution)/shard_map/reshape | solution.py:30
  279.0 7.6 convolution_convert_fusion
  286.6 12.5 copy.85
  299.1 29.4 %copy.87 = bf16[128,8,64,64]{2,3,1,0:T(8,128)(2,1)} copy(bf16[128,8,64,64]{0,3,2,1:T(8,128)(2,1)} %bitcast.86) | data formatting | bytes 16777216 | tf_op jit(solution)/shard_map/reshape | solution.py:30
  328.5 17.0 %fusion.34 = f32[128,8,64,64]{3,2,1,0:T(8,128)} fusion(bf16[128,8,64,64]{2,3,1,0:T(8,128)(2,1)} %copy.75, bf16[128,64,64,1]{2,1,3,0:T(8,128)(2,1)S(1)} %copy-done.2), kind=kOutput, calls=%fused_computation.78 | convolution fusion | flops 536870912 | bytes 26214400 | tf_op jit(solution)/shard_map/rax,rsxb->rsab/dot_general | solution.py:32
  345.5 17.0 %fusion.35 = f32[128,8,64,64]{3,2,1,0:T(8,128)} fusion(bf16[128,8,64,64]{2,3,1,0:T(8,128)(2,1)} %copy.79, bf16[128,64,64,1]{2,1,3,0:T(8,128)(2,1)S(1)} %copy-done.3), kind=kOutput, calls=%fused_computation.79 | convolution fusion | flops 536870912 | bytes 26214400 | tf_op jit(solution)/shard_map/rax,rsxb->rsab/dot_general | solution.py:32
  362.6 17.0 %fusion.36 = f32[128,8,64,64]{3,2,1,0:T(8,128)} fusion(bf16[128,8,64,64]{2,3,1,0:T(8,128)(2,1)} %copy.83, bf16[128,64,64,1]{2,1,3,0:T(8,128)(2,1)S(1)} %copy-done.4), kind=kOutput, calls=%fused_computation.80 | convolution fusion | flops 536870912 | bytes 26214400 | tf_op jit(solution)/shard_map/rax,rsxb->rsab/dot_general | solution.py:32
  379.6 48.7 %add_bitcast_fusion = f32[128,8,64,64]{2,3,1,0:T(8,128)} fusion(f32[128,8,64,64]{3,2,1,0:T(8,128)} %fusion.36, f32[128,8,64,64]{3,2,1,0:T(8,128)} %fusion.34, f32[128,8,64,64]{3,2,1,0:T(8,128)} %fusion.35, bf16[128,8,64,64]{2,3,1,0:T(8,128)(2,1)} %copy.87, bf16[128,64,64,1]{2,1,3,0:T(8,128)(2,1)S(1)} %copy-done.1), kind=kOutput, calls=%fused_computation.10 | convolution fusion | flops 549453824 | bytes 76546048 | tf_op jit(solution)/shard_map/rax,rsxb->rsab/dot_general | solution.py:32
  428.3 33.4 %copy.89 = f32[128,8,64,64]{3,2,1,0:T(8,128)} copy(f32[128,8,64,64]{2,3,1,0:T(8,128)} %add_bitcast_fusion) | data formatting | bytes 33554432 | tf_op jit(solution)/shard_map/add | solution.py:32
  461.8 27.9 %reshape.136 = f32[8,16,8,4096]{3,2,1,0:T(8,128)} reshape(f32[128,8,64,64]{3,2,1,0:T(8,128)} %copy.89) | data formatting | bytes 33554432 | tf_op jit(solution)/shard_map/reshape | solution.py:36
  489.7 365.8 %all-reduce.2 = bf16[8,16,8,4096]{3,2,1,0:T(8,128)(2,1)} all-reduce(f32[8,16,8,4096]{3,2,1,0:T(8,128)} %reshape.136), channel_id=2, replica_groups=mesh['row'=8,'col'=16] {'col'}, use_global_device_ids=true, to_apply=%region_0.3.clone | all-reduce | flops 4194304 | bytes 25165824
  855.5 1.7 dynamic-slice_convert_fusion
  857.2 1.1 reshape_squeeze.22
  858.3 4.5 convolution_bitcast_fusion
  862.8 9.2 copy.96
  872.0 7.9 reshape.216
  879.9 14.3 scatter_custom_fusion
  894.2 683.0 %reduce-scatter.3.cloned.1.call-done = f32[1,8,4096]{2,1,0:T(8,128)} async-done(((f32[128,8,4096]{2,1,0:T(8,128)}), f32[1,8,4096]{2,1,0:T(8,128)}) %reduce-scatter.3.cloned.1.call-update) | async-done | bytes 131088 | tf_op jit(solution)/shard_map/reduce_scatter | solution.py:63
  (41 shorter events, 0.4 us)
Async XLA Ops:
  7.2 79.9 %all-gather.2.cloned.1.call-start = ((), (), s32[]{:S(2)}) async-start(), calls=%async_computation.1 | async-start | bytes 2359296 | tf_op jit(solution)/shard_map/all_gather | solution.py:18
  7.9 1569.3 %reduce-scatter.3.cloned.1.call-start = ((), (), s32[]{:S(2)}) async-start(), calls=%async_computation.2 | async-start | bytes 16908288 | tf_op jit(solution)/shard_map/reduce_scatter | solution.py:63
  64.2 5.7 copy-start.8
  69.9 11.2 copy-start.7
  87.1 9.5 copy-start
  111.8 7.8 copy-start.12
  139.7 40.6 %copy-start.11 = (pred[128]{0:T(512)(128)(4,1)S(1)}, pred[128]{0:T(512)(128)(4,1)}, u32[]{:S(2)}) copy-start(pred[128]{0:T(512)(128)(4,1)} %get-tuple-element.16) | copy-start | bytes 388
  200.4 29.2 %copy-start.10 = (pred[128]{0:T(512)(128)(4,1)S(1)}, pred[128]{0:T(512)(128)(4,1)}, u32[]{:S(2)}) copy-start(pred[128]{0:T(512)(128)(4,1)} %get-tuple-element.20) | copy-start | bytes 388
  249.8 29.2 %copy-start.9 = (pred[128]{0:T(512)(128)(4,1)S(1)}, pred[128]{0:T(512)(128)(4,1)}, u32[]{:S(2)}) copy-start(pred[128]{0:T(512)(128)(4,1)} %get-tuple-element.4) | copy-start | bytes 388
  299.1 29.4 %copy-start.2 = (bf16[128,64,64,1]{2,1,3,0:T(8,128)(2,1)S(1)}, bf16[128,64,64,1]{2,1,3,0:T(8,128)(2,1)}, u32[]{:S(2)}) copy-start(bf16[128,64,64,1]{2,1,3,0:T(8,128)(2,1)} %copy.97) | copy-start | bytes 3145732
  328.5 17.0 %copy-start.3 = (bf16[128,64,64,1]{2,1,3,0:T(8,128)(2,1)S(1)}, bf16[128,64,64,1]{2,1,3,0:T(8,128)(2,1)}, u32[]{:S(2)}) copy-start(bf16[128,64,64,1]{2,1,3,0:T(8,128)(2,1)} %copy.98) | copy-start | bytes 3145732
  345.5 17.0 %copy-start.4 = (bf16[128,64,64,1]{2,1,3,0:T(8,128)(2,1)S(1)}, bf16[128,64,64,1]{2,1,3,0:T(8,128)(2,1)}, u32[]{:S(2)}) copy-start(bf16[128,64,64,1]{2,1,3,0:T(8,128)(2,1)} %copy.99) | copy-start | bytes 3145732
  362.6 17.0 %copy-start.1 = (bf16[128,64,64,1]{2,1,3,0:T(8,128)(2,1)S(1)}, bf16[128,64,64,1]{2,1,3,0:T(8,128)(2,1)}, u32[]{:S(2)}) copy-start(bf16[128,64,64,1]{2,1,3,0:T(8,128)(2,1)} %copy.100) | copy-start | bytes 3145732
  489.7 368.6 %copy-start.5 = (bf16[8,4,64,64,1]{3,2,1,0,4:T(8,128)(2,1)S(1)}, bf16[8,4,64,64,1]{3,2,1,0,4:T(8,128)(2,1)}, u32[]{:S(2)}) copy-start(bf16[8,4,64,64,1]{3,2,1,0,4:T(8,128)(2,1)} %reshape.250) | copy-start | bytes 786436
  857.2 5.7 copy-start.6
Sparse Core Ops, SparseCore 0:
  9.7 28.0 all-gather.1
  894.3 682.8 reduce-scatter.2
where the time goes:
time: 1600 us; the launch traced here: 1580 us
  waiting for transfers between devices  684 us (43%)
  blocking collectives  380 us (24%)
  local copies, waits for them, and re-layouts  352 us (22%)
  matrix products  135 us (8%)
  other arithmetic  19.3 us (1%)
    reduce_scatter x1, waiting for transfers between devices, shards(): lax.psum_scatter(coarse_terms, ('row', 'col'), scatter_dimension=0, tiled...  683 us
    unnamed x1, blocking collectives  366 us
    reshape x4, local copies, waits for them, and re-layouts, shards(): chosen = chosen.astype(jnp.bfloat16).reshape(row_count, KAP, B, B)  128 us
    dot_general x4, matrix products, shards(): jnp.einsum('rax,rsxb->rsab', jac_block, chosen, preferred_element_type=jn...  99.8 us
    convert_element_type x4, local copies, waits for them, and re-layouts, shards(): chosen = chosen.astype(jnp.bfloat16).reshape(row_count, KAP, B, B)  50 us
    add x1, local copies, waits for them, and re-layouts, shards(): partial_value + jnp.einsum('rax,rsxb->rsab', jac_block, chosen, preferred...  33.4 us
    gather x4, local copies, waits for them, and re-layouts, shards(): picked = jnp.take(group_vals, fine_cols, axis=0)  32.4 us
  transfers between devices with their start and end apart: 2, of which 1 were waited for; matrix products, arithmetic and copies ran while one was open for 4% of the time, Pallas kernels for 0%

commit v1 on v0

v1 whole, which is shorter than its diff:
```python
import jax
import jax.numpy as jnp
from jax import lax
from jax.experimental import pallas as pl
from jax.experimental.pallas import tpu as pltpu
from jax.sharding import PartitionSpec as P

B = 64
KA = 4
KP = 4
KAP = 8
KC = 8
NROW = 8
NCOL = 16
NK = 64
NCB = 128
CB = 4


def nt_dot(a, b):
    return lax.dot_general(a, b, (((1,), (1,)), ((), ())), preferred_element_type=jnp.float32)


def product_kernel(idx_ref, a_ref, pt_ref, out_ref, dup_ref, w_ref):
    ih = pl.program_id(0)
    qh = pl.program_id(1)
    cblk = pl.program_id(2)
    low = lax.broadcasted_iota(jnp.int32, (B, 128), 1) < B

    @pl.when((ih == 0) & (qh == 0) & (cblk == 0))
    def _():
        def fill(k, carry):
            for mh in range(2):
                v = pt_ref[k, :, mh * 128:(mh + 1) * 128]
                turned = jnp.concatenate([v[:, B:], v[:, :B]], axis=1)
                dup_ref[k * 4 + 2 * mh] = jnp.where(low, v, turned)
                dup_ref[k * 4 + 2 * mh + 1] = jnp.where(low, turned, v)
            return carry

        lax.fori_loop(0, NK, fill, 0)
        dup_ref[NK * KP] = jnp.zeros((B, 128), jnp.bfloat16)

    def pair(cc, carry):
        for lo in range(2):
            base = (((ih * 4 + qh * 2 + lo) * NCOL) + cblk * CB + cc) * (KA * KAP)
            for ep in range(2):
                for s in range(KAP):
                    first = dup_ref[idx_ref[base + (2 * ep) * KAP + s]]
                    second = dup_ref[idx_ref[base + (2 * ep + 1) * KAP + s]]
                    column = (lo * 2 + ep) * 128
                    w_ref[s * B:(s + 1) * B, column:column + 128] = jnp.where(low, first, second)
        zero = jnp.zeros((B, KA * B), jnp.bfloat16)
        stacked = jnp.concatenate(
            [
                jnp.concatenate([a_ref[0, 0, 0, cc], zero], axis=1),
                jnp.concatenate([zero, a_ref[0, 0, 1, cc]], axis=1),
            ],
            axis=0,
        )
        res = nt_dot(w_ref[...], stacked)
        for s in range(KAP):
            out_ref[:, 0, cc, 0, s] = res[s * B:(s + 1) * B].reshape(8, 8, 128)
        return carry

    lax.fori_loop(0, CB, pair, 0)


def products(idx, a, pt):
    return pl.pallas_call(
        product_kernel,
        grid_spec=pltpu.PrefetchScalarGridSpec(
            num_scalar_prefetch=1,
            grid=(2, 2, NCOL // CB),
            in_specs=[
                pl.BlockSpec((1, 1, 2, CB, B, KA * B), lambda ih, qh, c, idx: (ih, qh, 0, c, 0, 0)),
                pl.BlockSpec((NK, B, KP * B), lambda ih, qh, c, idx: (0, 0, 0)),
            ],
            out_specs=pl.BlockSpec(
                (8, 1, CB, 1, KAP, 8, 128), lambda ih, qh, c, idx: (0, ih, c, qh, 0, 0, 0)
            ),
            scratch_shapes=[
                pltpu.VMEM((NK * KP + 1, B, 128), jnp.bfloat16),
                pltpu.VMEM((KAP * B, 2 * KA * B), jnp.bfloat16),
            ],
        ),
        out_shape=jax.ShapeDtypeStruct((8, 2, NCOL, 2, KAP, 8, 128), jnp.float32),
        name="products",
    )(idx, a, pt)


def coarse_kernel(tgt_ref, half_ref, x_ref, p_ref, out_ref, acc_ref):
    c = pl.program_id(0)
    low = lax.broadcasted_iota(jnp.int32, (8, 128), 1) < B
    low_x = lax.broadcasted_iota(jnp.int32, (B, 128), 1) < B

    @pl.when(c == 0)
    def _():
        acc_ref[...] = jnp.zeros_like(acc_ref)

    for qh in range(2):
        x = x_ref[0, qh]
        none = jnp.zeros_like(x)
        lhs = jnp.concatenate([jnp.where(low_x, x, none), jnp.where(low_x, none, x)], axis=0)
        rhs = p_ref[0, 2 * qh:2 * qh + 2].reshape(2 * B, KP * B)
        res = lax.dot_general(
            lhs, rhs, (((1,), (0,)), ((), ())), preferred_element_type=jnp.float32
        )
        for lo in range(2):
            for m in range(KP):
                for s in range(KAP):
                    at = tgt_ref[(((c * 2 + qh) * 2 + lo) * KP + m) * KAP + s]
                    rows = (lo * KAP + s) * 8
                    tile = res[rows:rows + 8, (m // 2) * 128:(m // 2) * 128 + 128]
                    keep = low if m % 2 == 0 else jnp.logical_not(low)
                    acc_ref[at] = acc_ref[at] + jnp.where(keep, tile, 0.0)

    @pl.when(c == NCOL - 1)
    def _():
        def fold(j, carry):
            for tp in range(KC // 2):
                t0 = acc_ref[j * KC + 2 * tp]
                t1 = acc_ref[j * KC + 2 * tp + 1]
                t0 = t0 + pltpu.roll(t0, B, 1)
                t1 = t1 + pltpu.roll(t1, B, 1)
                out_ref[j, tp] = jnp.where(low, t0, t1)
            return carry

        lax.fori_loop(0, NCB, fold, 0)


def coarse_terms(tgt, half, x, p):
    return pl.pallas_call(
        coarse_kernel,
        grid_spec=pltpu.PrefetchScalarGridSpec(
            num_scalar_prefetch=2,
            grid=(NCOL,),
            in_specs=[
                pl.BlockSpec((1, 2, B, 128), lambda c, tgt, half: (c, 0, 0, 0)),
                pl.BlockSpec((1, 4, B, KP * B), lambda c, tgt, half: (c, half[0], 0, 0)),
            ],
            out_specs=pl.BlockSpec((NCB, KC // 2, 8, 128), lambda c, tgt, half: (0, 0, 0, 0)),
            scratch_shapes=[pltpu.VMEM((NCB * KC + 1, 8, 128), jnp.float32)],
        ),
        out_shape=jax.ShapeDtypeStruct((NCB, KC // 2, 8, 128), jnp.float32),
        name="coarse_terms",
    )(tgt, half, x, p)


def pick_rows(table, index):
    hot = (index[..., None] == jnp.arange(table.shape[0], dtype=jnp.int32)).astype(jnp.bfloat16)
    rows = jnp.einsum(
        "...k,km->...m", hot, table.astype(jnp.bfloat16), preferred_element_type=jnp.float32
    )
    return rows.astype(jnp.int32)


def shards(a_blocks, a_index, p_blocks, p_index, ap_index, coarse_index):
    own = p_blocks[:, 0].reshape(8, KP, B, B)
    pt = own.transpose(0, 3, 1, 2).reshape(8, B, KP * B)
    pn = own.transpose(0, 2, 1, 3).reshape(8, B, KP * B)
    ptg = lax.all_gather(pt, "row", axis=0, tiled=True)
    png = lax.all_gather(pn, "col", axis=0)
    cols_k = lax.all_gather(p_index[:, 0], "row", axis=0, tiled=True)
    cols_i = lax.all_gather(p_index[:, 0], "col", axis=1).reshape(128, KP)

    a_idx = a_index[:, 0]
    picked = pick_rows(cols_k, a_idx)
    equal = picked[:, :, None, :] == ap_index[:, None, :, None]
    ids = a_idx[:, :, None, None] * KP + jnp.arange(KP, dtype=jnp.int32)
    idx = jnp.min(jnp.where(equal, ids, NK * KP), axis=3).reshape(-1)

    a = a_blocks[:, 0].reshape(128, KA, B, B).transpose(0, 2, 1, 3).reshape(2, 2, 2, NCOL, B, KA * B)
    partial = products(idx, a, ptg)
    summed = lax.psum_scatter(
        partial.reshape(NCOL, NCOL, 2, KAP, 8, 128), "col", scatter_dimension=0, tiled=True
    )[0]
    apt = summed.astype(jnp.bfloat16)

    back = lax.all_to_all(apt, "col", 0, 0, tiled=True)
    ap_out = (
        back.reshape(8, 2, 2, KAP, 8, 2, B)
        .transpose(1, 2, 5, 3, 6, 0, 4)
        .reshape(8, 1, KAP, B * B)
    )

    half = lax.axis_index("col") % 2
    targets = pick_rows(coarse_index, cols_i)
    hit = targets[:, :, None, :] == ap_index[:, None, :, None]
    slot = cols_i[:, :, None, None] * KC + jnp.arange(KC, dtype=jnp.int32)
    tgt = jnp.min(jnp.where(hit, slot, NCB * KC), axis=3)
    tgt = tgt.reshape(2, 2, 2, NCOL, KP, KAP)
    tgt = lax.dynamic_index_in_dim(tgt, half, 0, keepdims=False)
    tgt = tgt.transpose(2, 0, 1, 3, 4).reshape(-1)
    coarse = coarse_terms(
        tgt, half.reshape(1).astype(jnp.int32), apt.reshape(NCOL, 2, KAP * 8, 128), png
    )
    coarse = lax.psum_scatter(
        coarse.reshape(NROW, NCOL, KC // 2, 8, 128), "row", scatter_dimension=0, tiled=True
    )[0]
    coarse = lax.all_to_all(coarse, "col", 0, 0, tiled=True)
    coarse = coarse.reshape(8, 2, KC // 2, 8, 2, B).sum(axis=1)
    coarse_out = coarse.transpose(1, 3, 4, 0, 2).reshape(1, KC, B * B)
    return ap_out, coarse_out


def solution(mesh):
    placed = (
        P("row", "col", None, None),
        P("row", "col", None),
        P("row", "col", None, None),
        P("row", "col", None),
        P("row", None),
        P(),
    )
    return jax.shard_map(
        shards,
        mesh=mesh,
        in_specs=placed,
        out_specs=(P("row", "col", None, None), P(("row", "col"), None, None)),
        check_vma=False,
    )
```

time: 1600 us -> 360 us (0.23)
  waiting for transfers between devices: 684 us -> 153 us
  blocking collectives: 380 us -> 54.8 us
  local copies, waits for them, and re-layouts: 352 us -> 64.9 us
  matrix products: 135 us -> 1.08 us
  Pallas kernels: 0 us -> 59 us
    reduce_scatter x1, waiting for transfers between devices: 683 us -> 18 us  [shards(): lax.psum_scatter(coarse.reshape(NROW, NCOL, KC // 2, 8, 128), 'row', scat...]
    unnamed x1 -> x0, blocking collectives: 366 us -> none
    dot_general x9 -> x2, matrix products: 135 us -> 1.08 us  [pick_rows(): jnp.einsum('...k,km->...m', hot, table.astype(jnp.bfloat16), preferred_el...]
    reshape x7 -> x9, local copies, waits for them, and re-layouts: 165 us -> 31.6 us  [the longest x1 13.5 us: shards(): ap_out = back.reshape(8, 2, 2, KAP, 8, 2, B).transpose(1, 2, 5, 3, 6, 0,...]
    unnamed x2 -> x5, waiting for transfers between devices: 0.7 us -> 84.7 us
    pallas_call x0 -> x2, Pallas kernels: none -> 59 us  [the longest x1 31.3 us: products(): pl.pallas_call(product_kernel, grid_spec=pltpu.PrefetchScalarGridSpec(num...]
    convert_element_type x5 -> x0, local copies, waits for them, and re-layouts: 51.7 us -> none  [the longest x4 50 us: shards(): chosen = chosen.astype(jnp.bfloat16).reshape(row_count, KAP, B, B)]
    all_gather x1 -> x2, waiting for transfers between devices: 0.02 us -> 50.5 us  [the longest x1 50.5 us: shards(): png = lax.all_gather(pn, 'col', axis=0)]
  transfers between devices with their start and end apart: 2 -> 5, of which waited for: 1 -> 3; matrix products, arithmetic and copies ran while one was open for 4% -> 18% of each run, Pallas kernels for 0% -> 0%
where the time goes in v1:
time: 360 us; the launch traced here: 358 us
  waiting for transfers between devices  153 us (42%)
  local copies, waits for them, and re-layouts  64.9 us (18%)
  Pallas kernels  59 us (16%)
  blocking collectives  54.8 us (15%)
  between operations  13.9 us (4%)
  starting transfers between devices  6.8 us (2%)
  other arithmetic  4.21 us (1%)
    unnamed x5, waiting for transfers between devices  84.7 us
    all_gather x1, waiting for transfers between devices, shards(): png = lax.all_gather(pn, 'col', axis=0)  50.5 us
    pallas_call x1, Pallas kernels, products(): pl.pallas_call(product_kernel, grid_spec=pltpu.PrefetchScalarGridSpec(num...  31.3 us
    pallas_call x1, Pallas kernels, coarse_terms(): pl.pallas_call(coarse_kernel, grid_spec=pltpu.PrefetchScalarGridSpec(num_...  27.7 us
    all_gather x1, blocking collectives, shards(): cols_i = lax.all_gather(p_index[:, 0], 'col', axis=1).reshape(128, KP)  24.2 us
    reduce_scatter x1, waiting for transfers between devices, shards(): lax.psum_scatter(coarse.reshape(NROW, NCOL, KC // 2, 8, 128), 'row', scat...  18 us
    all_to_all x1, blocking collectives, shards(): back = lax.all_to_all(apt, 'col', 0, 0, tiled=True)  16.3 us
    all_gather x1, blocking collectives, shards(): cols_k = lax.all_gather(p_index[:, 0], 'row', axis=0, tiled=True)  14.2 us
  transfers between devices with their start and end apart: 5, of which 3 were waited for; matrix products, arithmetic and copies ran while one was open for 18% of the time, Pallas kernels for 0%

profile of v1, /device:TPU:0, one launch (start us, length us, event | category | flops | bytes accessed | tf_op | source)
XLA Modules:
  0.0 357.8 jit_solution(6271146904170524486)
XLA Ops:
  7.2 0.0 all-gather.4.cloned.1.call-start
  7.2 1.4 reshape_squeeze.7
  8.6 0.3 copy.81
  8.9 1.0 reshape.79
  10.0 0.0 all-gather.4.cloned.1.call-update
  10.0 0.0 reduce-scatter.7.cloned.1.call-start
  10.1 0.8 copy.76
  10.8 14.2 %all-gather = s32[64,1,4]{2,1,0:T(1,128)S(1)} all-gather(s32[8,1,4]{2,1,0:T(1,128)S(1)} %copy.76), channel_id=2, replica_groups=mesh['row'=8,'col'=16] {'row'}, dimensions={0}, use_global_device_ids=true | all-gather | bytes 1152 | tf_op jit(solution)/shard_map/all_gather | solution.py:163
  25.0 0.1 copy.77
  25.1 0.7 broadcast_multiply_fusion.1
  25.8 0.8 convolution_convert_fusion.1
  26.6 0.7 select_reduce_fusion.1
  27.3 0.1 copy.78
  27.5 0.8 reshape.77.idx_ref
  28.3 7.8 %copy.79 = bf16[128,1,4,4096]{0,3,2,1:T(8,128)(2,1)} copy(bf16[128,1,4,4096]{3,2,1,0:T(4,128)(2,1)} %param.6) | data formatting | bytes 8388608 | tf_op args[0]
  36.2 13.8 %copy.80 = bf16[128,64,4,64]{3,2,1,0:T(4,128)(2,1)} copy(bf16[128,64,4,64]{0,3,1,2:T(8,128)(2,1)} %bitcast.46) | data formatting | bytes 8388608 | tf_op jit(solution)/shard_map/transpose | solution.py:172
  49.9 12.7 %reshape.78.a_ref = bf16[2,2,2,16,64,256]{5,4,3,2,1,0:T(8,128)(2,1)} reshape(bf16[128,64,4,64]{3,2,1,0:T(4,128)(2,1)} %copy.80) | data formatting | bytes 8388608 | tf_op jit(solution)/shard_map/reshape | solution.py:172
  62.6 0.0 all-gather.4.cloned.1.call-done.pt_ref
  62.6 31.3 %products.1 = f32[8,2,16,2,8,8,128]{6,5,4,3,2,1,0:T(8,128)} custom-call(s32[4096]{0:T(1024)} %reshape.77.idx_ref, bf16[2,2,2,16,64,256]{5,4,3,2,1,0:T(8,128)(2,1)} %reshape.78.a_ref, bf16[64,64,256]{2,1,0:T(8,128)(2,1)} %all-gather.4.cloned.1.call-done.pt_ref), custom_call_target="tpu_custom_call" | custom-call | tf_op jit(solution)/shard_map/products/pallas_call | solution.py:69
  93.9 0.0 copy-start.1
  93.9 0.0 copy-start.2
  93.9 0.0 copy-start
  93.9 0.0 reduce-scatter.7.cloned.1.call-update
  93.9 0.0 all-gather.6.cloned.1.call-start
  94.0 0.4 copy.91
  94.4 1.0 all_gather_reshape.3
  95.4 0.0 all-gather.6.cloned.1.call-update
  95.5 0.0 reduce-scatter.5.cloned.1.call-start
  95.5 0.0 copy-done.1
  95.5 24.2 %all_gather.14 = s32[8,16,4]{0,2,1:T(4,128)S(1)} all-gather(s32[8,1,4]{0,2,1:T(4,128)S(1)} %copy-done.1), channel_id=1, replica_groups=mesh['row'=8,'col'=16] {'col'}, dimensions={1}, use_global_device_ids=true | all-gather | bytes 2176 | tf_op jit(solution)/shard_map/all_gather | solution.py:164
  119.8 0.1 copy.83
  119.9 0.1 eq.65
  120.0 0.0 copy-done.2
  120.0 0.3 convolution_convert_fusion
  120.2 0.0 copy-done
  120.2 0.1 select_reduce_fusion
  120.3 0.2 reshape.83
  120.6 0.1 copy.85
  120.7 0.8 reshape.84.tgt_ref
  121.5 84.6 %reduce-scatter.7.cloned.1.call-done = f32[1,16,2,8,8,128]{5,4,3,2,1,0:T(8,128)} async-done(((f32[16,16,2,8,8,128]{5,4,3,2,1,0:T(8,128)}), f32[1,16,2,8,8,128]{5,4,3,2,1,0:T(8,128)}) %reduce-scatter.7.cloned.1.call-update) | async-done | bytes 1048592
  206.1 2.3 convert_bitcast_fusion
  208.4 50.5 %all-gather.6.cloned.1.call-done.p_ref = bf16[16,8,64,256]{3,2,1,0:T(8,128)(2,1)} async-done(((bf16[1,8,64,256]{3,2,1,0:T(8,128)(2,1)}), bf16[16,8,64,256]{3,2,1,0:T(8,128)(2,1)}) %all-gather.6.cloned.1.call-update) | async-done | bytes 4194320 | tf_op jit(solution)/shard_map/all_gather | solution.py:162
  258.8 27.7 %coarse_terms.1 = f32[128,4,8,128]{3,2,1,0:T(8,128)} custom-call(s32[2048]{0:T(1024)} %reshape.84.tgt_ref, s32[1]{0:T(128)} %bitcast.13.half_ref, bf16[16,2,64,128]{3,2,1,0:T(8,128)(2,1)} %get-tuple-element.12.x_ref, bf16[16,8,64,256]{3,2,1,0:T(8,128)(2,1)} %all-gather.6.cloned.1.call-done.p_ref), custom_call_target="tpu_custom_call" | custom-call | tf_op jit(solution)/shard_map/coarse_terms/pallas_call | solution.py:132
  286.5 0.0 reduce-scatter.5.cloned.1.call-update
  286.5 16.3 %all_to_all.10 = bf16[16,2,8,8,128]{4,3,2,1,0:T(8,128)(2,1)S(1)} all-to-all(bf16[16,2,8,8,128]{4,3,2,1,0:T(8,128)(2,1)S(1)} %get-tuple-element.13), channel_id=1, replica_groups=mesh['row'=8,'col'=16] {'col'}, dimensions={0} | all-to-all | bytes 1048576 | tf_op jit(solution)/shard_map/all_to_all | solution.py:179
  302.9 18.0 %reduce-scatter.5.cloned.1.call-done = f32[1,16,4,8,128]{4,3,2,1,0:T(8,128)} async-done(((f32[8,16,4,8,128]{4,3,2,1,0:T(8,128)}), f32[1,16,4,8,128]{4,3,2,1,0:T(8,128)}) %reduce-scatter.5.cloned.1.call-update) | async-done | bytes 262160 | tf_op jit(solution)/shard_map/reduce_scatter | solution.py:197
  320.9 6.6 %all-to-all-start.1 = ((f32[16,4,8,128]{3,2,1,0:T(8,128)}), f32[16,4,8,128]{3,2,1,0:T(8,128)S(1)}, u32[]{:S(2)}, u32[]{:S(2)}) async-start(f32[16,4,8,128]{3,2,1,0:T(8,128)} %bitcast.54), calls=%async_computation.2 | async-start | bytes 524288 | tf_op jit(solution)/shard_map/all_to_all | solution.py:200
  327.5 0.4 reshape.81
  327.9 6.5 %copy.82 = bf16[2,2,2,8,64,8,8]{6,5,4,3,2,1,0:T(8,128)(2,1)} copy(bf16[2,2,2,8,64,8,8]{4,2,6,3,1,0,5:T(2,128)(2,1)S(1)} %bitcast.48) | data formatting | bytes 1048576 | tf_op jit(solution)/shard_map/transpose | solution.py:182
  334.4 13.5 %reshape.82 = bf16[8,1,8,4096]{3,2,0,1:T(8,128)(2,1)} reshape(bf16[2,2,2,8,64,8,8]{6,5,4,3,2,1,0:T(8,128)(2,1)} %copy.82) | data formatting | bytes 1048576 | tf_op jit(solution)/shard_map/reshape | solution.py:183
  347.9 0.0 all-to-all-done.1
  347.9 0.3 reshape.87
  348.3 0.4 reduce_sum.9
  348.7 0.7 copy.87
  349.4 1.8 reshape.88
  (5 shorter events, 0.0 us)
Async XLA Ops:
  7.2 55.5 %all-gather.4.cloned.1.call-start = ((), (), s32[]{:S(2)}) async-start(), calls=%async_computation.4 | async-start | bytes 2359296 | tf_op jit(solution)/shard_map/all_gather | solution.py:161
  10.0 196.1 %reduce-scatter.7.cloned.1.call-start = ((), (), s32[]{:S(2)}) async-start(), calls=%async_computation.7 | async-start | bytes 17825792
  93.9 1.6 copy-start.1
  93.9 26.1 %copy-start.2 = (s32[128,8]{0,1:T(8,128)S(1)}, s32[128,8]{0,1:T(8,128)}, u32[]{:S(2)}) copy-start(s32[128,8]{0,1:T(8,128)} %param.11) | copy-start | bytes 12292
  93.9 26.3 %copy-start = (s32[128,8]{0,1:T(8,128)S(1)}, s32[128,8]{0,1:T(8,128)}, u32[]{:S(2)}) copy-start(s32[128,8]{0,1:T(8,128)} %param.10) | copy-start | bytes 12292
  93.9 164.9 %all-gather.6.cloned.1.call-start = ((), (), s32[]{:S(2)}) async-start(), calls=%async_computation.5 | async-start | bytes 4456448 | tf_op jit(solution)/shard_map/all_gather | solution.py:162
  95.5 225.4 %reduce-scatter.5.cloned.1.call-start = ((), (), s32[]{:S(2)}) async-start(), calls=%async_computation.6 | async-start | bytes 2359296 | tf_op jit(solution)/shard_map/reduce_scatter | solution.py:197
  320.9 27.1 %all-to-all-start.1 = ((f32[16,4,8,128]{3,2,1,0:T(8,128)}), f32[16,4,8,128]{3,2,1,0:T(8,128)S(1)}, u32[]{:S(2)}, u32[]{:S(2)}) async-start(f32[16,4,8,128]{3,2,1,0:T(8,128)} %bitcast.54), calls=%async_computation.2 | async-start | bytes 524288 | tf_op jit(solution)/shard_map/all_to_all | solution.py:200
Sparse Core Ops, SparseCore 0:
  10.3 27.9 all-gather.3
  94.1 111.9 reduce-scatter.6
  208.2 50.5 all-gather.5
  286.7 34.1 reduce-scatter.4
